TPU v7x, 32 devices: a whole 2x2x4 slice. The times are simulated.
32 devices in a mesh: pair: 16 (over z, y, x), dp: 2 (over core).
Axes of the slice: x: 2, y: 2, z: 4, core: 2. Of those that a mesh axis runs over, the one named last changes fastest.
Arguments:
- features: bfloat16 [16384, 2048], P(('pair', 'dp')), may hold values from -6 to 6
- proj_weight: bfloat16 [2048, 128], replicated, may hold values from -0.01171875 to 0.01171875
- row_lse: bfloat16 [16384], P(('pair', 'dp')), may hold values from 6 to 9
- positive: int32 [16384], P(('pair', 'dp')), may hold values from 0 to 16383, as said below
Outputs:
- grad_embed: float32 [16384, 128], P(('pair', 'dp'))
- grad_weight: float32 [2048, 128], P('dp')
Inputs may be any that keep to these rules, and one draw needn't show every extreme that they name: positive[i] names the row that holds the other view of row i's cutout: positive[positive[i]] = i and positive[i] != i.
All inputs are finite; a program needn't handle non-finite values.
Results may differ from a plain program's by a relative error of at most 0.0045.
Values may be sent and summed in bfloat16 or wider, within the bound.
No kernel may reach another device: no remote copies, remote signals or barrier semaphores. Data moves between devices by JAX's collectives and lax.ppermute only.
A program may use at most 64 MiB of HBM per device.

v0:
```python
import jax
import jax.numpy as jnp
from jax import lax
from jax.sharding import PartitionSpec as P

contrastive_divisor = 0.1
epsilon = 1e-06


def from_behind(value, axis, steps):
    count = lax.axis_size(axis)
    pairs = [(source, (source + steps) % count) for source in range(count)]
    return lax.ppermute(value, axis, pairs)


def coupling_tile(embedded, own_lse, own_positive, counterpart_feature_vectors, part_lse, first_id):
    cosine_affinity_matrix = (
        lax.dot_general(
            embedded,
            counterpart_feature_vectors,
            (((1,), (1,)), ((), ())),
            preferred_element_type=jnp.float32,
        )
        / contrastive_divisor
    )
    weights = jnp.exp(cosine_affinity_matrix - own_lse.astype(jnp.float32)[:, None]) + jnp.exp(
        cosine_affinity_matrix - part_lse.astype(jnp.float32)[None, :]
    )
    identity_rows = first_id + jnp.arange(counterpart_feature_vectors.shape[0], dtype=jnp.int32)
    matched = (own_positive[:, None] == identity_rows[None, :]).astype(jnp.float32)
    return (weights - 2.0 * matched).astype(jnp.bfloat16)


def body(features, proj_weight, row_lse, positive):
    row_count = features.shape[0]
    dp_count = lax.axis_size("dp")
    pair_count = lax.axis_size("pair")
    group_rows = row_count * dp_count
    far_offset = pair_count // 4
    my_block = lax.axis_index("pair")
    projected = jnp.dot(features, proj_weight, preferred_element_type=jnp.float32)
    magnitude = jnp.sqrt(jnp.sum(projected * projected, axis=-1, keepdims=True) + epsilon)
    unit_vectors = projected / magnitude
    embedded = unit_vectors.astype(jnp.bfloat16)
    whole_embed, whole_lse = (
        lax.all_gather(embedded, "dp", axis=0, tiled=True),
        lax.all_gather(row_lse, "dp", axis=0, tiled=True),
    )
    upstream_derivative = jnp.zeros((row_count, embedded.shape[1]), jnp.float32)
    for offset in (1, far_offset):
        counterpart_feature_vectors, part_lse = from_behind(
            (whole_embed, whole_lse), "pair", offset
        )
        part_block = jnp.remainder(my_block - offset, pair_count)
        tile_coupling = coupling_tile(
            embedded,
            row_lse,
            positive,
            counterpart_feature_vectors,
            part_lse,
            part_block * group_rows,
        )
        coupling, counterpart_feature_vectors = (tile_coupling, counterpart_feature_vectors)
        upstream_derivative = upstream_derivative + jnp.dot(
            coupling, counterpart_feature_vectors, preferred_element_type=jnp.float32
        )
        returned = lax.psum_scatter(
            lax.dot_general(
                coupling, embedded, (((0,), (0,)), ((), ())), preferred_element_type=jnp.float32
            ),
            "dp",
            scatter_dimension=0,
            tiled=True,
        )
        upstream_derivative = upstream_derivative + from_behind(returned, "pair", -offset)
    derivative_pair_affinity = upstream_derivative / contrastive_divisor
    grad_embed = (
        derivative_pair_affinity
        - unit_vectors * jnp.sum(unit_vectors * derivative_pair_affinity, axis=-1, keepdims=True)
    ) / magnitude
    grad_half = grad_embed.astype(jnp.bfloat16)
    local_term = lax.dot_general(
        features, grad_half, (((0,), (0,)), ((), ())), preferred_element_type=jnp.float32
    )
    summed = lax.psum(local_term, "pair")
    grad_weight = lax.psum_scatter(summed, "dp", scatter_dimension=0, tiled=True)
    return (grad_embed, grad_weight)


def solution(mesh):
    return jax.shard_map(
        body,
        mesh=mesh,
        in_specs=(P(("pair", "dp"), None), P(), P(("pair", "dp")), P(("pair", "dp"))),
        out_specs=(P(("pair", "dp"), None), P("dp", None)),
        check_vma=False,
    )
```

profile of v0, /device:TPU:0, one launch (start us, length us, event | category | flops | bytes accessed | tf_op | source)
XLA Modules:
  0.0 204.0 jit_solution(16239086399272684663)
XLA Ops:
  7.2 1.5 copy-done
  8.8 1.9 multiply_reduce_fusion.1
  10.7 2.1 %all_gather.6 = bf16[1024,128]{0,1:T(8,128)(2,1)S(1)} all-gather(bf16[512,128]{0,1:T(8,128)(2,1)S(1)} %fusion.4), channel_id=1, replica_groups=mesh['pair'=16,'dp'=2] {'dp'}, dimensions={0}, use_global_device_ids=true | all-gather | bytes 393216 | tf_op jit(solution)/shard_map/all_gather | solution.py:46
  12.8 2.9 %collective-permute-start.3 = (bf16[1024,128]{0,1:T(8,128)(2,1)S(1)}, bf16[1024,128]{0,1:T(8,128)(2,1)S(1)}, u32[]{:S(2)}, u32[]{:S(2)}) collective-permute-start(bf16[1024,128]{0,1:T(8,128)(2,1)S(1)} %all_gather.6), channel_id=1, source_target_pairs={{0,8},{2,10},{4,12},{6,14},{8,16},{10,18},{12,20},{14,22},{16,24},... | collective-permute-start | bytes 786440 | tf_op jit(solution)/shard_map/ppermute | solution.py:13
  15.7 1.8 all-gather
  17.5 1.6 collective-permute-start.4
  19.2 1.5 collective-permute-start.1
  20.7 1.5 collective-permute-start
  22.1 2.3 %collective-permute-done.4 = bf16[1024]{0:T(1024)(128)(2,1)S(1)} collective-permute-done((bf16[1024]{0:T(1024)(128)(2,1)S(1)}, bf16[1024]{0:T(1024)(128)(2,1)S(1)}, u32[]{:S(2)}, u32[]{:S(2)}) %collective-permute-start.4) | collective-permute-done | bytes 2080 | tf_op jit(solution)/shard_map/ppermute | solution.py:13
  24.4 1.9 collective-permute-done.1
  26.8 5.3 %collective-permute-done = bf16[1024,128]{0,1:T(8,128)(2,1)S(1)} collective-permute-done((bf16[1024,128]{0,1:T(8,128)(2,1)S(1)}, bf16[1024,128]{0,1:T(8,128)(2,1)S(1)}, u32[]{:S(2)}, u32[]{:S(2)}) %collective-permute-start) | collective-permute-done | bytes 262176 | tf_op jit(solution)/shard_map/ppermute | solution.py:13
  32.8 3.0 %subtract_convert_fusion.1 = (bf16[512,1024]{1,0:T(8,128)(2,1)S(1)}, bf16[512,1024]{1,0:T(8,128)(2,1)S(1)}) fusion(s32[1024]{0:T(1024)S(1)} %get-tuple-element.15, f32[1024]{0:T(1024)S(1)} %convert_element_type.26, f32[512]{0:T(512)S(1)} %convert_element_type.25, s32[512]{0:T(512)S(1)} %copy-done.5, s32[1024]{0:T(1024)S(1)} %get-tuple-element.14, ...), kind=kOutput, calls=%fused_computation.2 | convolution fusion | flops 142606336 | bytes 4608000 | tf_op jit(solution)/shard_map/dot_general | solution.py:18
  37.9 1.1 fusion.7
  39.1 4.2 %reduce-scatter.6.cloned.1.call-done = f32[512,128]{0,1:T(8,128)} async-done(((f32[1024,128]{0,1:T(8,128)}), f32[512,128]{0,1:T(8,128)}) %reduce-scatter.6.cloned.1.call-update) | async-done | bytes 262160 | tf_op jit(solution)/shard_map/reduce_scatter | solution.py:67
  43.4 3.6 %collective-permute-start.5 = (f32[512,128]{0,1:T(8,128)}, f32[512,128]{0,1:T(8,128)}, u32[]{:S(2)}, u32[]{:S(2)}) collective-permute-start(f32[512,128]{0,1:T(8,128)} %reduce-scatter.6.cloned.1.call-done), channel_id=1, source_target_pairs={{0,24},{2,26},{4,28},{6,30},{8,0},{10,2},{12,4},{14,6},{16,8},{18,... | collective-permute-start | bytes 786440 | tf_op jit(solution)/shard_map/ppermute | solution.py:13
  46.9 7.9 %reduce-scatter.4.cloned.1.call-done = f32[512,128]{0,1:T(8,128)} async-done(((f32[1024,128]{0,1:T(8,128)}), f32[512,128]{0,1:T(8,128)}) %reduce-scatter.4.cloned.1.call-update) | async-done | bytes 262160 | tf_op jit(solution)/shard_map/reduce_scatter | solution.py:67
  54.8 5.4 %collective-permute-start.2 = (f32[512,128]{0,1:T(8,128)}, f32[512,128]{0,1:T(8,128)S(1)}, u32[]{:S(2)}, u32[]{:S(2)}) collective-permute-start(f32[512,128]{0,1:T(8,128)} %reduce-scatter.4.cloned.1.call-done), channel_id=1, source_target_pairs={{0,30},{2,0},{4,2},{6,4},{8,6},{10,8},{12,10},{14,12},{16,14},{18,... | collective-permute-start | bytes 786440 | tf_op jit(solution)/shard_map/ppermute | solution.py:13
  60.2 1.7 fusion.6
  62.0 4.6 %collective-permute-done.2 = f32[512,128]{0,1:T(8,128)S(1)} collective-permute-done((f32[512,128]{0,1:T(8,128)}, f32[512,128]{0,1:T(8,128)S(1)}, u32[]{:S(2)}, u32[]{:S(2)}) %collective-permute-start.2) | collective-permute-done | bytes 262176 | tf_op jit(solution)/shard_map/ppermute | solution.py:13
  66.6 1.6 multiply_reduce_fusion
  68.2 1.4 convolution_bitcast_fusion
  69.7 10.4 %reduce-scatter.8.cloned.1.call-done = f32[1024,128]{0,1:T(8,128)} async-done(((f32[2048,128]{0,1:T(8,128)}), f32[1024,128]{0,1:T(8,128)}) %reduce-scatter.8.cloned.1.call-update) | async-done | bytes 524304 | tf_op jit(solution)/shard_map/reduce_scatter | solution.py:86
  80.9 114.5 %all-reduce.2.cloned.1.call-done = f32[1024,128]{0,1:T(8,128)} async-done(((f32[1024,128]{0,1:T(8,128)}), f32[1024,128]{0,1:T(8,128)}) %all-reduce.2.cloned.1.call-update) | async-done | bytes 524304 | tf_op jit(solution)/shard_map/psum | solution.py:85
  195.4 2.0 copy.17
  (34 shorter events, 4.4 us)
Async XLA Ops:
  7.2 1.6 copy-start
  7.2 8.5 %copy-start.4 = (bf16[512]{0:T(512)(128)(2,1)S(1)}, bf16[512]{0:T(512)(128)(2,1)}, u32[]{:S(2)}) copy-start(bf16[512]{0:T(512)(128)(2,1)} %param.6) | copy-start | bytes 3076
  7.2 36.2 %reduce-scatter.6.cloned.1.call-start = ((), (), s32[]{:S(2)}) async-start(), calls=%async_computation.4 | async-start | bytes 786432 | tf_op jit(solution)/shard_map/reduce_scatter | solution.py:67
  10.6 22.2 %copy-start.5 = (s32[512]{0:T(512)S(1)}, s32[512]{0:T(512)}, u32[]{:S(2)}) copy-start(s32[512]{0:T(512)} %param.7) | copy-start | bytes 6148
  12.8 13.6 %collective-permute-start.3 = (bf16[1024,128]{0,1:T(8,128)(2,1)S(1)}, bf16[1024,128]{0,1:T(8,128)(2,1)S(1)}, u32[]{:S(2)}, u32[]{:S(2)}) collective-permute-start(bf16[1024,128]{0,1:T(8,128)(2,1)S(1)} %all_gather.6), channel_id=1, source_target_pairs={{0,8},{2,10},{4,12},{6,14},{8,16},{10,18},{12,20},{14,22},{16,24},... | collective-permute-start | bytes 786440 | tf_op jit(solution)/shard_map/ppermute | solution.py:13
  17.5 6.9 %collective-permute-start.4 = (bf16[1024]{0:T(1024)(128)(2,1)S(1)}, bf16[1024]{0:T(1024)(128)(2,1)S(1)}, u32[]{:S(2)}, u32[]{:S(2)}) collective-permute-start(bf16[1024]{0:T(1024)(128)(2,1)S(1)} %bitcast.20), channel_id=1, source_target_pairs={{0,8},{2,10},{4,12},{6,14},{8,16},{10,18},{12,20},{14,22},{16,24},... | collective-permute-start | bytes 6152 | tf_op jit(solution)/shard_map/ppermute | solution.py:13
  19.2 7.2 %collective-permute-start.1 = (bf16[1024]{0:T(1024)(128)(2,1)S(1)}, bf16[1024]{0:T(1024)(128)(2,1)S(1)}, u32[]{:S(2)}, u32[]{:S(2)}) collective-permute-start(bf16[1024]{0:T(1024)(128)(2,1)S(1)} %bitcast.21), channel_id=1, source_target_pairs={{0,2},{2,4},{4,6},{6,8},{8,10},{10,12},{12,14},{14,16},{16,18},{18... | collective-permute-start | bytes 6152 | tf_op jit(solution)/shard_map/ppermute | solution.py:13
  20.7 11.5 %collective-permute-start = (bf16[1024,128]{0,1:T(8,128)(2,1)S(1)}, bf16[1024,128]{0,1:T(8,128)(2,1)S(1)}, u32[]{:S(2)}, u32[]{:S(2)}) collective-permute-start(bf16[1024,128]{0,1:T(8,128)(2,1)S(1)} %all_gather.6), channel_id=1, source_target_pairs={{0,2},{2,4},{4,6},{6,8},{8,10},{10,12},{12,14},{14,16},{16,18},{18... | collective-permute-start | bytes 786440 | tf_op jit(solution)/shard_map/ppermute | solution.py:13
  26.3 5.8 %copy-start.2 = (bf16[1024,128]{0,1:T(8,128)(2,1)}, bf16[1024,128]{0,1:T(8,128)(2,1)S(1)}, u32[]{:S(2)}) copy-start(bf16[1024,128]{0,1:T(8,128)(2,1)S(1)} %collective-permute-done.3) | copy-start | bytes 786436
  32.1 0.7 copy-start.3
  35.8 1.0 copy-start.1
  37.9 17.0 %reduce-scatter.4.cloned.1.call-start = ((), (), s32[]{:S(2)}) async-start(), calls=%async_computation.3 | async-start | bytes 786432 | tf_op jit(solution)/shard_map/reduce_scatter | solution.py:67
  39.1 41.0 %reduce-scatter.8.cloned.1.call-start = ((), (), s32[]{:S(2)}) async-start(), calls=%async_computation.5 | async-start | bytes 1572864 | tf_op jit(solution)/shard_map/reduce_scatter | solution.py:86
  43.4 18.6 %collective-permute-start.5 = (f32[512,128]{0,1:T(8,128)}, f32[512,128]{0,1:T(8,128)}, u32[]{:S(2)}, u32[]{:S(2)}) collective-permute-start(f32[512,128]{0,1:T(8,128)} %reduce-scatter.6.cloned.1.call-done), channel_id=1, source_target_pairs={{0,24},{2,26},{4,28},{6,30},{8,0},{10,2},{12,4},{14,6},{16,8},{18,... | collective-permute-start | bytes 786440 | tf_op jit(solution)/shard_map/ppermute | solution.py:13
  54.8 11.7 %collective-permute-start.2 = (f32[512,128]{0,1:T(8,128)}, f32[512,128]{0,1:T(8,128)S(1)}, u32[]{:S(2)}, u32[]{:S(2)}) collective-permute-start(f32[512,128]{0,1:T(8,128)} %reduce-scatter.4.cloned.1.call-done), channel_id=1, source_target_pairs={{0,30},{2,0},{4,2},{6,4},{8,6},{10,8},{12,10},{14,12},{16,14},{18,... | collective-permute-start | bytes 786440 | tf_op jit(solution)/shard_map/ppermute | solution.py:13
  69.6 125.8 %all-reduce.2.cloned.1.call-start = ((), (), s32[]{:S(2)}) async-start(), calls=%async_computation.6 | async-start | bytes 1048576 | tf_op jit(solution)/shard_map/psum | solution.py:85
Sparse Core Ops, SparseCore 0:
  38.0 5.3 reduce-scatter.5
  45.7 9.1 reduce-scatter.3
  69.8 10.2 reduce-scatter.7
  85.9 109.4 all-reduce.1
where the time goes:
time: 204 us
  waiting for transfers between devices  151 us (74%)
  starting transfers between devices  16.6 us (8%)
  between operations  13.9 us (7%)
  matrix products  12.2 us (6%)
  local copies, waits for them, and re-layouts  6.09 us (3%)
  blocking collectives  3.86 us (2%)
    psum x1, waiting for transfers between devices, body(): summed = lax.psum(local_term, 'pair')  114 us
    ppermute x6, starting transfers between devices, from_behind(): return lax.ppermute(value, axis, pairs)  16.5 us
    ppermute x6, waiting for transfers between devices, from_behind(): return lax.ppermute(value, axis, pairs)  14.1 us
    reduce_scatter x2, waiting for transfers between devices, body(): lax.psum_scatter(lax.dot_general(coupling, embedded, (((0,), (0,)), ((),...  12.2 us
    reduce_scatter x1, waiting for transfers between devices, body(): lax.psum_scatter(summed, 'dp', scatter_dimension=0, tiled=True)  10.4 us
    unnamed x16, local copies, waits for them, and re-layouts  6.09 us
  transfers between devices with their start and end apart: 10, of which 8 were waited for; matrix products, arithmetic and copies ran while one was open for 2% of the time, Pallas kernels for 0%

commit v1 on v0

--- a/solution.py
+++ b/solution.py
@@ -82,7 +82,9 @@
     local_term = lax.dot_general(
         features, grad_half, (((0,), (0,)), ((), ())), preferred_element_type=jnp.float32
     )
-    summed = lax.psum(local_term, "pair")
+    summed = local_term
+    for hop in (1, 2, 4, 8):
+        summed = summed + lax.ppermute(summed, "pair", [(dev, dev ^ hop) for dev in range(16)])
     grad_weight = lax.psum_scatter(summed, "dp", scatter_dimension=0, tiled=True)
     return (grad_embed, grad_weight)
 

time: 204 us -> 206 us (level)
  starting transfers between devices: 16.6 us -> 20.6 us
  waiting for transfers between devices: 151 us -> 148 us
    psum x1 -> x0, waiting for transfers between devices: 114 us -> none  [body(): summed = lax.psum(local_term, 'pair')]
    ppermute x0 -> x4, waiting for transfers between devices: none -> 114 us  [body(): lax.ppermute(summed, 'pair', [(dev, dev ^ hop) for dev in range(16)])]
    ppermute x0 -> x4, starting transfers between devices: none -> 4.03 us  [body(): lax.ppermute(summed, 'pair', [(dev, dev ^ hop) for dev in range(16)])]
    reduce_scatter x1, waiting for transfers between devices: 10.4 us -> 7.99 us  [body(): lax.psum_scatter(summed, 'dp', scatter_dimension=0, tiled=True)]
  transfers between devices with their start and end apart: 10 -> 13, of which waited for: 8 -> 11; matrix products, arithmetic and copies ran while one was open for 2% -> 2% of each run, Pallas kernels for 0% -> 0%
where the time goes in v1:
time: 206 us
  waiting for transfers between devices  148 us (72%)
  starting transfers between devices  20.6 us (10%)
  between operations  13.9 us (7%)
  matrix products  11.3 us (5%)
  local copies, waits for them, and re-layouts  6.09 us (3%)
  blocking collectives  3.86 us (2%)
    ppermute x4, waiting for transfers between devices, body(): lax.ppermute(summed, 'pair', [(dev, dev ^ hop) for dev in range(16)])  114 us
    ppermute x6, starting transfers between devices, from_behind(): return lax.ppermute(value, axis, pairs)  16.5 us
    ppermute x6, waiting for transfers between devices, from_behind(): return lax.ppermute(value, axis, pairs)  14.1 us
    reduce_scatter x2, waiting for transfers between devices, body(): lax.psum_scatter(lax.dot_general(coupling, embedded, (((0,), (0,)), ((),...  12.1 us
    reduce_scatter x1, waiting for transfers between devices, body(): lax.psum_scatter(summed, 'dp', scatter_dimension=0, tiled=True)  7.99 us
    unnamed x16, local copies, waits for them, and re-layouts  6.09 us
  transfers between devices with their start and end apart: 13, of which 11 were waited for; matrix products, arithmetic and copies ran while one was open for 2% of the time, Pallas kernels for 0%

profile of v1, /device:TPU:0, one launch (start us, length us, event | category | flops | bytes accessed | tf_op | source)
XLA Modules:
  0.0 205.7 jit_solution(5898423274914004291)
XLA Ops:
  7.2 1.5 copy-done
  8.8 1.9 multiply_reduce_fusion.1
  10.7 2.1 %all_gather.6 = bf16[1024,128]{0,1:T(8,128)(2,1)S(1)} all-gather(bf16[512,128]{0,1:T(8,128)(2,1)S(1)} %fusion.4), channel_id=1, replica_groups=mesh['pair'=16,'dp'=2] {'dp'}, dimensions={0}, use_global_device_ids=true | all-gather | bytes 393216 | tf_op jit(solution)/shard_map/all_gather | solution.py:46
  12.8 2.9 %collective-permute-start.3 = (bf16[1024,128]{0,1:T(8,128)(2,1)S(1)}, bf16[1024,128]{0,1:T(8,128)(2,1)S(1)}, u32[]{:S(2)}, u32[]{:S(2)}) collective-permute-start(bf16[1024,128]{0,1:T(8,128)(2,1)S(1)} %all_gather.6), channel_id=1, source_target_pairs={{0,8},{2,10},{4,12},{6,14},{8,16},{10,18},{12,20},{14,22},{16,24},... | collective-permute-start | bytes 786440 | tf_op jit(solution)/shard_map/ppermute | solution.py:13
  15.7 1.8 all-gather
  17.5 1.6 collective-permute-start.4
  22.1 2.3 %collective-permute-done.4 = bf16[1024]{0:T(1024)(128)(2,1)S(1)} collective-permute-done((bf16[1024]{0:T(1024)(128)(2,1)S(1)}, bf16[1024]{0:T(1024)(128)(2,1)S(1)}, u32[]{:S(2)}, u32[]{:S(2)}) %collective-permute-start.4) | collective-permute-done | bytes 2080 | tf_op jit(solution)/shard_map/ppermute | solution.py:13
  24.4 1.9 collective-permute-done.1
  26.8 5.3 %collective-permute-done = bf16[1024,128]{0,1:T(8,128)(2,1)S(1)} collective-permute-done((bf16[1024,128]{0,1:T(8,128)(2,1)S(1)}, bf16[1024,128]{0,1:T(8,128)(2,1)S(1)}, u32[]{:S(2)}, u32[]{:S(2)}) %collective-permute-start) | collective-permute-done | bytes 262176 | tf_op jit(solution)/shard_map/ppermute | solution.py:13
  32.8 3.0 %subtract_convert_fusion.1 = (bf16[512,1024]{1,0:T(8,128)(2,1)S(1)}, bf16[512,1024]{1,0:T(8,128)(2,1)S(1)}) fusion(s32[1024]{0:T(1024)S(1)} %get-tuple-element.15, f32[1024]{0:T(1024)S(1)} %convert_element_type.26, f32[512]{0:T(512)S(1)} %convert_element_type.25, s32[512]{0:T(512)S(1)} %copy-done.5, s32[1024]{0:T(1024)S(1)} %get-tuple-element.14, ...), kind=kOutput, calls=%fused_computation.2 | convolution fusion | flops 142606336 | bytes 4608000 | tf_op jit(solution)/shard_map/dot_general | solution.py:18
  39.1 4.2 %reduce-scatter.6.cloned.1.call-done = f32[512,128]{0,1:T(8,128)} async-done(((f32[1024,128]{0,1:T(8,128)}), f32[512,128]{0,1:T(8,128)}) %reduce-scatter.6.cloned.1.call-update) | async-done | bytes 262160 | tf_op jit(solution)/shard_map/reduce_scatter | solution.py:67
  43.4 3.5 %collective-permute-start.5 = (f32[512,128]{0,1:T(8,128)}, f32[512,128]{0,1:T(8,128)}, u32[]{:S(2)}, u32[]{:S(2)}) collective-permute-start(f32[512,128]{0,1:T(8,128)} %reduce-scatter.6.cloned.1.call-done), channel_id=1, source_target_pairs={{0,24},{2,26},{4,28},{6,30},{8,0},{10,2},{12,4},{14,6},{16,8},{18,... | collective-permute-start | bytes 786440 | tf_op jit(solution)/shard_map/ppermute | solution.py:13
  46.9 7.9 %reduce-scatter.4.cloned.1.call-done = f32[512,128]{0,1:T(8,128)} async-done(((f32[1024,128]{0,1:T(8,128)}), f32[512,128]{0,1:T(8,128)}) %reduce-scatter.4.cloned.1.call-update) | async-done | bytes 262160 | tf_op jit(solution)/shard_map/reduce_scatter | solution.py:67
  54.8 5.4 %collective-permute-start.2 = (f32[512,128]{0,1:T(8,128)}, f32[512,128]{0,1:T(8,128)S(1)}, u32[]{:S(2)}, u32[]{:S(2)}) collective-permute-start(f32[512,128]{0,1:T(8,128)} %reduce-scatter.4.cloned.1.call-done), channel_id=1, source_target_pairs={{0,30},{2,0},{4,2},{6,4},{8,6},{10,8},{12,10},{14,12},{16,14},{18,... | collective-permute-start | bytes 786440 | tf_op jit(solution)/shard_map/ppermute | solution.py:13
  60.2 1.7 fusion.6
  62.0 4.6 %collective-permute-done.2 = f32[512,128]{0,1:T(8,128)S(1)} collective-permute-done((f32[512,128]{0,1:T(8,128)}, f32[512,128]{0,1:T(8,128)S(1)}, u32[]{:S(2)}, u32[]{:S(2)}) %collective-permute-start.2) | collective-permute-done | bytes 262176 | tf_op jit(solution)/shard_map/ppermute | solution.py:13
  66.6 1.6 multiply_reduce_fusion
  68.7 24.6 %collective-permute-done.6 = f32[2048,128]{0,1:T(8,128)S(1)} collective-permute-done((f32[2048,128]{0,1:T(8,128)S(1)}, f32[2048,128]{0,1:T(8,128)S(1)}, u32[]{:S(2)}, u32[]{:S(2)}) %collective-permute-start.6) | collective-permute-done | bytes 1048608 | tf_op jit(solution)/shard_map/ppermute | solution.py:87
  93.7 23.5 %collective-permute-done.7 = f32[2048,128]{0,1:T(8,128)S(1)} collective-permute-done((f32[2048,128]{0,1:T(8,128)S(1)}, f32[2048,128]{0,1:T(8,128)S(1)}, u32[]{:S(2)}, u32[]{:S(2)}) %collective-permute-start.7) | collective-permute-done | bytes 1048608 | tf_op jit(solution)/shard_map/ppermute | solution.py:87
  117.6 22.5 %collective-permute-done.8 = f32[2048,128]{0,1:T(8,128)S(1)} collective-permute-done((f32[2048,128]{0,1:T(8,128)S(1)}, f32[2048,128]{0,1:T(8,128)S(1)}, u32[]{:S(2)}, u32[]{:S(2)}) %collective-permute-start.8) | collective-permute-done | bytes 1048608 | tf_op jit(solution)/shard_map/ppermute | solution.py:87
  140.3 3.4 %collective-permute-start.9 = (f32[2048,128]{0,1:T(8,128)S(1)}, f32[2048,128]{0,1:T(8,128)S(1)}, u32[]{:S(2)}, u32[]{:S(2)}) collective-permute-start(f32[2048,128]{0,1:T(8,128)S(1)} %add.88), channel_id=1, source_target_pairs={{0,16},{2,18},{4,20},{6,22},{8,24},{10,26},{12,28},{14,30},{16,0},... | collective-permute-start | bytes 3145736 | tf_op jit(solution)/shard_map/ppermute | solution.py:87
  143.7 43.4 %collective-permute-done.9 = f32[2048,128]{0,1:T(8,128)S(1)} collective-permute-done((f32[2048,128]{0,1:T(8,128)S(1)}, f32[2048,128]{0,1:T(8,128)S(1)}, u32[]{:S(2)}, u32[]{:S(2)}) %collective-permute-start.9) | collective-permute-done | bytes 1048608 | tf_op jit(solution)/shard_map/ppermute | solution.py:87
  189.1 8.0 %reduce-scatter.8.cloned.1.call-done = f32[1024,128]{0,1:T(8,128)} async-done(((f32[2048,128]{0,1:T(8,128)}), f32[1024,128]{0,1:T(8,128)}) %reduce-scatter.8.cloned.1.call-update) | async-done | bytes 524304 | tf_op jit(solution)/shard_map/reduce_scatter | solution.py:88
  197.1 2.0 copy.17
  (43 shorter events, 11.0 us)
Async XLA Ops:
  7.2 1.6 copy-start
  7.2 8.5 %copy-start.4 = (bf16[512]{0:T(512)(128)(2,1)S(1)}, bf16[512]{0:T(512)(128)(2,1)}, u32[]{:S(2)}) copy-start(bf16[512]{0:T(512)(128)(2,1)} %param.6) | copy-start | bytes 3076
  7.2 36.2 %reduce-scatter.6.cloned.1.call-start = ((), (), s32[]{:S(2)}) async-start(), calls=%async_computation.4 | async-start | bytes 786432 | tf_op jit(solution)/shard_map/reduce_scatter | solution.py:67
  10.6 22.2 %copy-start.5 = (s32[512]{0:T(512)S(1)}, s32[512]{0:T(512)}, u32[]{:S(2)}) copy-start(s32[512]{0:T(512)} %param.7) | copy-start | bytes 6148
  12.8 13.6 %collective-permute-start.3 = (bf16[1024,128]{0,1:T(8,128)(2,1)S(1)}, bf16[1024,128]{0,1:T(8,128)(2,1)S(1)}, u32[]{:S(2)}, u32[]{:S(2)}) collective-permute-start(bf16[1024,128]{0,1:T(8,128)(2,1)S(1)} %all_gather.6), channel_id=1, source_target_pairs={{0,8},{2,10},{4,12},{6,14},{8,16},{10,18},{12,20},{14,22},{16,24},... | collective-permute-start | bytes 786440 | tf_op jit(solution)/shard_map/ppermute | solution.py:13
  17.5 6.9 %collective-permute-start.4 = (bf16[1024]{0:T(1024)(128)(2,1)S(1)}, bf16[1024]{0:T(1024)(128)(2,1)S(1)}, u32[]{:S(2)}, u32[]{:S(2)}) collective-permute-start(bf16[1024]{0:T(1024)(128)(2,1)S(1)} %bitcast.20), channel_id=1, source_target_pairs={{0,8},{2,10},{4,12},{6,14},{8,16},{10,18},{12,20},{14,22},{16,24},... | collective-permute-start | bytes 6152 | tf_op jit(solution)/shard_map/ppermute | solution.py:13
  19.2 7.2 %collective-permute-start.1 = (bf16[1024]{0:T(1024)(128)(2,1)S(1)}, bf16[1024]{0:T(1024)(128)(2,1)S(1)}, u32[]{:S(2)}, u32[]{:S(2)}) collective-permute-start(bf16[1024]{0:T(1024)(128)(2,1)S(1)} %bitcast.21), channel_id=1, source_target_pairs={{0,2},{2,4},{4,6},{6,8},{8,10},{10,12},{12,14},{14,16},{16,18},{18... | collective-permute-start | bytes 6152 | tf_op jit(solution)/shard_map/ppermute | solution.py:13
  20.7 11.5 %collective-permute-start = (bf16[1024,128]{0,1:T(8,128)(2,1)S(1)}, bf16[1024,128]{0,1:T(8,128)(2,1)S(1)}, u32[]{:S(2)}, u32[]{:S(2)}) collective-permute-start(bf16[1024,128]{0,1:T(8,128)(2,1)S(1)} %all_gather.6), channel_id=1, source_target_pairs={{0,2},{2,4},{4,6},{6,8},{8,10},{10,12},{12,14},{14,16},{16,18},{18... | collective-permute-start | bytes 786440 | tf_op jit(solution)/shard_map/ppermute | solution.py:13
  26.3 5.8 %copy-start.2 = (bf16[1024,128]{0,1:T(8,128)(2,1)}, bf16[1024,128]{0,1:T(8,128)(2,1)S(1)}, u32[]{:S(2)}) copy-start(bf16[1024,128]{0,1:T(8,128)(2,1)S(1)} %collective-permute-done.3) | copy-start | bytes 786436
  32.1 0.7 copy-start.3
  35.8 1.0 copy-start.1
  37.9 16.9 %reduce-scatter.4.cloned.1.call-start = ((), (), s32[]{:S(2)}) async-start(), calls=%async_computation.3 | async-start | bytes 786432 | tf_op jit(solution)/shard_map/reduce_scatter | solution.py:67
  39.1 158.0 %reduce-scatter.8.cloned.1.call-start = ((), (), s32[]{:S(2)}) async-start(), calls=%async_computation.5 | async-start | bytes 1572864 | tf_op jit(solution)/shard_map/reduce_scatter | solution.py:88
  43.4 18.6 %collective-permute-start.5 = (f32[512,128]{0,1:T(8,128)}, f32[512,128]{0,1:T(8,128)}, u32[]{:S(2)}, u32[]{:S(2)}) collective-permute-start(f32[512,128]{0,1:T(8,128)} %reduce-scatter.6.cloned.1.call-done), channel_id=1, source_target_pairs={{0,24},{2,26},{4,28},{6,30},{8,0},{10,2},{12,4},{14,6},{16,8},{18,... | collective-permute-start | bytes 786440 | tf_op jit(solution)/shard_map/ppermute | solution.py:13
  54.8 11.8 %collective-permute-start.2 = (f32[512,128]{0,1:T(8,128)}, f32[512,128]{0,1:T(8,128)S(1)}, u32[]{:S(2)}, u32[]{:S(2)}) collective-permute-start(f32[512,128]{0,1:T(8,128)} %reduce-scatter.4.cloned.1.call-done), channel_id=1, source_target_pairs={{0,30},{2,0},{4,2},{6,4},{8,6},{10,8},{12,10},{14,12},{16,14},{18,... | collective-permute-start | bytes 786440 | tf_op jit(solution)/shard_map/ppermute | solution.py:13
  68.7 24.7 %collective-permute-start.6 = (f32[2048,128]{0,1:T(8,128)S(1)}, f32[2048,128]{0,1:T(8,128)S(1)}, u32[]{:S(2)}, u32[]{:S(2)}) collective-permute-start(f32[2048,128]{0,1:T(8,128)S(1)} %convolution_bitcast_fusion), channel_id=1, source_target_pairs={{0,2},{2,0},{4,6},{6,4},{8,10},{10,8},{12,14},{14,12},{16,18},{18,... | collective-permute-start | bytes 3145736 | tf_op jit(solution)/shard_map/ppermute | solution.py:87
  93.5 23.7 %collective-permute-start.7 = (f32[2048,128]{0,1:T(8,128)S(1)}, f32[2048,128]{0,1:T(8,128)S(1)}, u32[]{:S(2)}, u32[]{:S(2)}) collective-permute-start(f32[2048,128]{0,1:T(8,128)S(1)} %add.86), channel_id=1, source_target_pairs={{0,4},{2,6},{4,0},{6,2},{8,12},{10,14},{12,8},{14,10},{16,20},{18,... | collective-permute-start | bytes 3145736 | tf_op jit(solution)/shard_map/ppermute | solution.py:87
  117.3 22.8 %collective-permute-start.8 = (f32[2048,128]{0,1:T(8,128)S(1)}, f32[2048,128]{0,1:T(8,128)S(1)}, u32[]{:S(2)}, u32[]{:S(2)}) collective-permute-start(f32[2048,128]{0,1:T(8,128)S(1)} %add.87), channel_id=1, source_target_pairs={{0,8},{2,10},{4,12},{6,14},{8,0},{10,2},{12,4},{14,6},{16,24},{18,... | collective-permute-start | bytes 3145736 | tf_op jit(solution)/shard_map/ppermute | solution.py:87
  140.3 46.9 %collective-permute-start.9 = (f32[2048,128]{0,1:T(8,128)S(1)}, f32[2048,128]{0,1:T(8,128)S(1)}, u32[]{:S(2)}, u32[]{:S(2)}) collective-permute-start(f32[2048,128]{0,1:T(8,128)S(1)} %add.88), channel_id=1, source_target_pairs={{0,16},{2,18},{4,20},{6,22},{8,24},{10,26},{12,28},{14,30},{16,0},... | collective-permute-start | bytes 3145736 | tf_op jit(solution)/shard_map/ppermute | solution.py:87
Sparse Core Ops, SparseCore 0:
  38.0 5.3 reduce-scatter.5
  45.7 9.0 reduce-scatter.3
  188.4 8.6 reduce-scatter.7
